TPU v7x, 32 devices: a whole 2x2x4 slice. The times are simulated.
32 devices in a mesh: case: 4 (over z), span: 2 (over x), vert: 4 (over y, core).
Axes of the slice: x: 2, y: 2, z: 4, core: 2. Of those that a mesh axis runs over, the one named last changes fastest.
Arguments:
- state: float32 [8, 4, 16, 32, 512], P('case', None, 'span', 'vert'), may hold values from -3 to 4.5
- turbine_x: int32 [8, 6], P('case'), may hold values from 128 to 511
- turbine_y: int32 [8, 6], P('case'), may hold values from 0 to 15
- yaw_index: int32 [8], P('case'), may hold values from 0 to 7
Outputs:
- final_state: float32 [8, 4, 16, 32, 512], P('case', None, 'span', 'vert')
All inputs are finite; a program needn't handle non-finite values.
Results may differ from a plain program's by a relative error of at most 0.0003.
Values sent between devices are 32-bit elements; how exact they have to be, the bound alone decides.
No kernel may reach another device: no remote copies, remote signals or barrier semaphores. Data moves between devices by JAX's collectives and lax.ppermute only.
A program may use at most 64 MiB of HBM per device.

v0:
```python
import functools

import jax
import jax.numpy as jnp
from jax import lax
from jax.experimental import pallas as pl
from jax.experimental.pallas import tpu as pltpu
from jax.sharding import PartitionSpec as P

STEPS = 3
DISK = 8
LANES = 128
HALO = 2 * STEPS

U_MEAN = 1.0
VISC = 0.04
THRUST = 0.75
TIME_STEP = 0.1
YAW_STEP = 0.15
HALF = 0.5 * TIME_STEP
SCALES = (HALF * HALF, HALF, HALF, HALF)

ROW0 = 8
STRIP = 16


def flat(blocks):
    _, z, x = blocks.shape[-3:]
    a = blocks.reshape(-1, z, x // LANES, LANES)
    return jnp.swapaxes(a, 1, 2).reshape(-1, LANES)


def unflat(rows, shape):
    _, z, x = shape[-3:]
    a = rows.reshape(-1, x // LANES, z, LANES)
    return jnp.swapaxes(a, 1, 2).reshape(shape)


def away_kernel(dims, state_ref, near_ref, far_ref, block, sem):
    fields, ry, rz, tiles = dims
    size = fields * ry * tiles * rz
    slot = 1 - lax.axis_index("span")
    even = lax.axis_index("vert") % 2 == 0
    start = pl.multiple_of(slot * size, 8)
    copy = pltpu.make_async_copy(state_ref.at[pl.ds(start, size)], block, sem)
    copy.start()
    copy.wait()
    near = jnp.where(even, 0, rz - HALO)
    far = jnp.where(even, HALO, 0)
    for ref, low, count in ((near_ref, near, HALO), (far_ref, far, rz - HALO)):
        for f in range(fields):
            for t in range(tiles):
                for k in range(count):
                    row = (f * ry * tiles + t) * rz + low + k
                    value = block[pl.ds(row, ry, stride=tiles * rz), :]
                    ref[pl.ds(((f * tiles + t) * count + k) * ry, ry), :] = value


def own_kernel(dims, state_ref, after_ref, own_ref, near_ref, fringe_ref, block, first, sems):
    del after_ref
    fields, ry, rz, tiles = dims
    size = fields * ry * tiles * rz
    slot = lax.axis_index("span")
    even = lax.axis_index("vert") % 2 == 0
    start = pl.multiple_of(slot * size, 8)
    copy_first = pltpu.make_async_copy(state_ref.at[pl.ds(0, size)], first, sems.at[0])
    copy_own = pltpu.make_async_copy(state_ref.at[pl.ds(start, size)], block, sems.at[1])
    copy_first.start()
    copy_own.start()
    copy_first.wait()
    lane = lax.broadcasted_iota(jnp.int32, (ry, LANES), 1)
    for f in range(fields):
        strip = jnp.zeros((ry, LANES), jnp.float32)
        for z in range(rz):
            row = f * ry * tiles * rz + z
            step = tiles * rz
            place = f * (rz + 1) + z
            fringe_ref[pl.ds(place * ry, ry), :] = first[pl.ds(row, ry, stride=step), :]
            after = first[pl.ds(row + rz, ry, stride=step), :]
            before = first[pl.ds(row + (tiles - 1) * rz, ry, stride=step), :]
            both = jnp.where(lane < LANES // 2, after, before)
            both = pltpu.roll(both, (HALO + STRIP * z) % LANES, 1)
            here = (lane >= STRIP * z) & (lane < STRIP * z + 2 * HALO)
            strip = jnp.where(here, both, strip)
        fringe_ref[pl.ds((f * (rz + 1) + rz) * ry, ry), :] = strip
    copy_own.wait()
    for f in range(fields):
        for t in range(tiles):
            for z in range(rz):
                row = (f * ry * tiles + t) * rz + z
                value = block[pl.ds(row, ry, stride=tiles * rz), :]
                own_ref[pl.ds(((f * tiles + t) * rz + z) * ry, ry), :] = value
    near = jnp.where(even, 0, rz - HALO)
    for c in range(fields * tiles):
        for k in range(HALO):
            row = pl.multiple_of((c * rz + near + k) * ry, 8)
            near_ref[pl.ds((c * HALO + k) * ry, ry), :] = own_ref[pl.ds(row, ry), :]


def main_kernel(
    dims, xs, ys, yaws, own, got_near, got_far, out_own, out_got, in_own, in_near, in_far,
    p_own, p_got, p_out_own, p_out_got, p_in_own, p_in_got,
    mine_ref, send_ref, q, m, pq, pm, wgt, sides0, sides1,
):
    fields, ry, rz, tiles, nt, slots = dims
    ext = rz + 2 * HALO
    rows = ext + 2
    total_y = 2 * ry
    total_z = rz * lax.axis_size("vert")
    store = 2 * ROW0 + total_y
    groups = total_y // 8
    slot = lax.axis_index("span")
    vert_at = lax.axis_index("vert")
    z0 = vert_at * rz
    even = vert_at % 2 == 0
    dlo = jnp.maximum(HALO - z0, 0)
    dhi = jnp.minimum(HALO + total_z - z0, ext)
    gate = HALO + total_z // 2 - z0
    y_off = slot * ry
    one = 1 + jnp.minimum(vert_at, 0)
    active = jnp.where(lax.axis_index("case") * slots + slot > 0, 1.0, 0.0)
    lane = lax.broadcasted_iota(jnp.int32, (8, LANES), 1)
    sub = lax.broadcasted_iota(jnp.int32, (8, LANES), 0)
    first_lane = lane == 0
    last_lane = lane == LANES - 1
    angle = (jnp.full((8, LANES), yaws[slot], jnp.int32).astype(jnp.float32) - 3.5) * YAW_STEP
    cos_yaw = jnp.cos(angle)
    sin_yaw = jnp.sin(angle)
    ramp = 0.5 * (1.0 - jnp.cos(jnp.pi * (lane.astype(jnp.float32) + 1.0) / LANES))

    def put(dst, width, f, t, z, group, value):
        start = pl.multiple_of(((f * width + t) * rows + z + 1) * store, 8)
        dst[pl.ds(start + (ROW0 + 8 * group), 8), :] = value
        if group == 0:
            dst[pl.ds(start + (ROW0 + total_y), 1), :] = value[0:1]
        if group == groups - 1:
            dst[pl.ds(start + (ROW0 - 1), 1), :] = value[7:8]

    def scale_of(f):
        return jnp.where(f == 0, SCALES[0], SCALES[1])

    def fill(parts):
        def one_field(f, carry):
            for src, held, taken, half, z_dst, count in parts:
                for t in range(tiles):
                    for k in range(count):
                        row = pl.multiple_of(((f * tiles + t) * held + taken + k) * ry, 8)
                        for g in range(ry // 8):
                            value = scale_of(f) * src[pl.ds(row + 8 * g, 8), :]
                            put(q, tiles, f, t, z_dst + k, half * (ry // 8) + g, value)
            return carry

        lax.fori_loop(0, fields, one_field, 0)

    def fill_fringe(parts):
        def one_field(f, carry):
            for src, taken, half, z_dst, count in parts:
                base = f * (rz + 1)
                strip = scale_of(f) * src[pl.ds(pl.multiple_of((base + rz) * ry, 8), ry), :]
                for k in range(count):
                    z = taken + k
                    row = pl.multiple_of((base + z) * ry, 8)
                    put(pq, 2, f, 0, z_dst + k, half, scale_of(f) * src[pl.ds(row, ry), :])
                    value = pltpu.roll(strip, 2 * LANES - HALO - STRIP * z, 1)
                    put(pq, 2, f, 1, z_dst + k, half, value)
            return carry

        lax.fori_loop(0, fields, one_field, 0)

    def pick(a, b):
        return jnp.where(even, a, b)

    above = HALO + rz
    rest = rz - HALO
    fill(
        (
            (own, rz, 0, 0, HALO, rz),
            (in_own, rz, pick(0, rest), 0, pick(above, 0), HALO),
            (out_own, HALO, 0, 0, pick(0, above), HALO),
        )
    )
    fill(
        (
            (got_near, HALO, 0, 1, HALO + pick(0, rest), HALO),
            (got_far, rest, 0, 1, HALO + pick(HALO, 0), rest),
            (out_got, HALO, 0, 1, pick(0, above), HALO),
            (in_near, HALO, pick(0, rest), 1, pick(above + rest, 0), HALO - rest),
            (in_far, rest, 0, 1, pick(above, HALO - rest), rest),
        )
    )
    fill_fringe(
        (
            (p_own, 0, 0, HALO, rz),
            (p_got, 0, 1, HALO, rz),
            (p_out_own, pick(rest, 0), 0, pick(0, above), HALO),
            (p_out_got, pick(rest, 0), 1, pick(0, above), HALO),
            (p_in_own, pick(0, rest), 0, pick(above, 0), HALO),
            (p_in_got, pick(0, rest), 1, pick(above, 0), HALO),
        )
    )

    zero = jnp.zeros((store, LANES), jnp.float32)
    for ref, width in ((m, tiles), (pm, 2), (q, tiles), (pq, 2)):
        for z in (HALO - 1, HALO + rz):
            outside = (z < dlo) | (z >= dhi)

            def clear(ref=ref, width=width, z=z):
                for f in range(fields):
                    for t in range(width):
                        ref[pl.ds(((f * width + t) * rows + z + 1) * store, store), :] = zero

            pl.when(outside)(clear)

    for t in range(1, tiles):
        for g in range(groups):
            acc = jnp.zeros((8, LANES), jnp.float32)
            y = y_off + 8 * g + sub
            for k in range(nt):
                hit = lax.rem(y - ys[slot, k] + 2 * total_y, total_y) < DISK
                hit = hit & (lane + t * LANES == xs[slot, k])
                acc = acc + jnp.where(hit, 1.0, 0.0)
            acc = acc * active
            wgt[0, 0, t, g] = jnp.zeros((8, LANES), jnp.float32)
            wgt[0, 1, t, g] = jnp.zeros((8, LANES), jnp.float32)
            wgt[1, 0, t, g] = acc * (2.0 * THRUST * cos_yaw)
            wgt[1, 1, t, g] = acc * (2.0 * THRUST * sin_yaw)

    def stage(src, base, dst, width, k, is_domain):
        second = k % 2 == 0

        def at(ref, f, t, g, z, dy=0):
            start = ((f * width + t % width) * rows + z + 1) * store + ROW0 + 8 * g
            start = start + dy * one if dy else pl.multiple_of(start, 8)
            return ref[pl.ds(start, 8), :]

        def beside(f, t, g, side):
            return pl.ds((((f * 2 + side) * width + t) * groups + g) * 8, 8)

        def shift(z, into, t, g):
            for f in range(fields):
                c = at(src, f, t, g, z)
                after = at(src, f, t + 1, g, z)
                before = at(src, f, t - 1, g, z)
                east = pltpu.roll(jnp.where(first_lane, after, c), LANES - 1, 1)
                west = pltpu.roll(jnp.where(last_lane, before, c), 1, 1)
                into[beside(f, t, g, 0), :] = east
                into[beside(f, t, g, 1), :] = west

        def row(z, sides, following):
            if is_domain:
                on = jnp.where(z < gate, 1, 0)
            for t in range(width):
                for g in range(groups):
                    shift(z + 1, following, t, g)
                    c = [at(src, f, t, g, z) for f in range(fields)]
                    gx, gy, gz, lap = [], [], [], []
                    for f in range(fields):
                        east = sides[beside(f, t, g, 0), :]
                        west = sides[beside(f, t, g, 1), :]
                        north = at(src, f, t, g, z, dy=1)
                        south = at(src, f, t, g, z, dy=-1)
                        upper = at(src, f, t, g, z + 1)
                        lower = at(src, f, t, g, z - 1)
                        gx.append(east - west)
                        gy.append(north - south)
                        gz.append(upper - lower)
                        around = ((east + west) + (north + south)) + (upper + lower)
                        lap.append(around - 6.0 * c[f])
                    speed = c[1] + HALF * U_MEAN
                    strain = gx[1] * gx[1] + gy[2] * gy[2] + gz[3] * gz[3]
                    strain = strain + gy[1] * gy[1] + gz[1] * gz[1] + 4.0 * HALF * HALF
                    viscous = VISC * (strain * lax.rsqrt(strain))
                    rate = [
                        viscous * lap[f] - (speed * gx[f] + c[2] * gy[f] + c[3] * gz[f])
                        for f in range(fields)
                    ]
                    rate[0] = rate[0] - HALF * HALF * (gx[1] + gy[2] + gz[3])
                    rate[1] = rate[1] - gx[0]
                    rate[2] = rate[2] - gy[0]
                    rate[3] = rate[3] - gz[0]
                    if is_domain and t > 0:
                        normal = speed * cos_yaw + c[2] * sin_yaw
                        thrust = normal * jnp.abs(normal)
                        rate[1] = rate[1] - thrust * wgt[on, 0, t, g]
                        rate[2] = rate[2] - thrust * wgt[on, 1, t, g]
                    for f in range(fields):
                        if second:
                            new = 0.5 * ((at(base, f, t, g, z) + c[f]) + rate[f])
                            if is_domain and t == 0:
                                start = pl.multiple_of((f * 2 * rows + z + 1) * store, 8)
                                new = new + ramp * (pq[pl.ds(start + (ROW0 + 8 * g), 8), :] - new)
                        else:
                            new = c[f] + rate[f]
                        if is_domain and k == HALO:
                            out = mine_ref if g < groups // 2 else send_ref
                            start = ((f * tiles + t) * rz + z - HALO) * ry + 8 * (g % (groups // 2))
                            new = new * (1.0 / SCALES[f])
                            out[pl.ds(pl.multiple_of(start, 8), 8), :] = new
                        else:
                            put(dst, width, f, t, z, g, new)

        first = jnp.maximum(k, dlo)
        count = jnp.minimum(ext - k, dhi) - first
        first = first - jnp.where(dhi < ext, count & 1, 0)
        for t in range(width):
            for g in range(groups):
                shift(first, sides0, t, g)

        def pair(i, carry):
            z = first + 2 * i
            row(z, sides0, sides1)
            row(z + 1, sides1, sides0)
            return carry

        lax.fori_loop(0, (count + 1) // 2, pair, 0)

    for step in range(STEPS):
        k = 2 * step + 1
        stage(pq, None, pm, 2, k, False)
        stage(pm, pq, pq, 2, k + 1, False)
        stage(q, None, m, tiles, k, True)
        stage(m, q, q, tiles, k + 1, True)


def place_kernel(dims, other, *refs):
    fields, ry, rz, tiles = dims
    src, out_ref, block, sems = refs[0], refs[-3], refs[-2], refs[-1]
    size = ry * tiles * rz
    slot = lax.axis_index("span")
    slot = 1 - slot if other else slot
    copies = []
    for f in range(fields):
        for y in range(ry):
            for t in range(tiles):
                value = src[pl.ds((f * tiles + t) * rz * ry + y, rz, stride=ry), :]
                block[pl.ds(((f * ry + y) * tiles + t) * rz, rz), :] = value
        start = pl.multiple_of((slot * fields + f) * size, 8)
        part = block.at[pl.ds(f * size, size)]
        copies.append(pltpu.make_async_copy(part, out_ref.at[pl.ds(start, size)], sems.at[f]))
        copies[-1].start()
    for copy in copies:
        copy.wait()


def swaps(size):
    inner = [(i, i ^ 1) for i in range(size)]
    outer = [(i, i + 1 if i % 2 else i - 1) for i in range(size)]
    outer = [(i, j) for i, j in outer if 0 <= j < size]
    return inner, outer


def spread(value, axis):
    size = lax.axis_size(axis)
    at = lax.axis_index(axis)
    gap = size // 2
    while gap:
        pairs = [(i, i + gap) for i in range(0, size, 2 * gap)]
        moved = lax.ppermute(value, axis, pairs)
        value = jnp.where(at % (2 * gap) == gap, moved, value)
        gap //= 2
    return value


def body(state, turbine_x, turbine_y, yaw_index):
    slots, fields, ry, rz, x = state.shape
    tiles = x // LANES
    nt = turbine_x.shape[1]
    count = fields * ry * tiles * rz
    near_count = count // rz * HALO
    fringe_count = fields * (rz + 1) * ry
    dims = (fields, ry, rz, tiles)
    inner, outer = swaps(lax.axis_size("vert"))
    across = [(0, 1), (1, 0)]
    smem = pl.BlockSpec(memory_space=pltpu.SMEM)
    vmem = pl.BlockSpec(memory_space=pltpu.VMEM)
    hbm = pl.BlockSpec(memory_space=pl.ANY)
    whole = flat(state)

    def rows_of(n):
        return jax.ShapeDtypeStruct((n, LANES), jnp.float32)

    def block_of(n):
        return pltpu.VMEM((n, LANES), jnp.float32)

    away_near, away_far = pl.pallas_call(
        functools.partial(away_kernel, dims),
        out_shape=[rows_of(near_count), rows_of(count - near_count)],
        in_specs=[hbm],
        out_specs=[vmem, vmem],
        scratch_shapes=[block_of(count), pltpu.SemaphoreType.DMA],
        compiler_params=pltpu.CompilerParams(vmem_limit_bytes=8 << 20),
        name="away",
    )(whole)
    got_near = lax.ppermute(away_near, "span", across)
    got_far = lax.ppermute(away_far, "span", across)
    own, near, fringe = pl.pallas_call(
        functools.partial(own_kernel, dims),
        out_shape=[rows_of(count), rows_of(near_count), rows_of(fringe_count)],
        in_specs=[hbm, hbm],
        out_specs=[vmem, vmem, vmem],
        scratch_shapes=[block_of(count), block_of(count), pltpu.SemaphoreType.DMA((2,))],
        compiler_params=pltpu.CompilerParams(vmem_limit_bytes=8 << 20),
        name="own",
    )(whole, away_far)
    out_own = lax.ppermute(near, "vert", outer)
    in_own = lax.ppermute(own, "vert", inner)
    fringe = spread(fringe, "case")
    fringe_got = lax.ppermute(fringe, "span", across)
    out_got = lax.ppermute(got_near, "vert", outer)
    in_near = lax.ppermute(got_near, "vert", inner)
    in_far = lax.ppermute(got_far, "vert", inner)
    fringes = [fringe, fringe_got]
    for pairs in (outer, inner):
        for a in (fringe, fringe_got):
            fringes.append(lax.ppermute(a, "vert", pairs))

    ext = rz + 2 * HALO
    store = 2 * ROW0 + 2 * ry
    mine, send = pl.pallas_call(
        functools.partial(main_kernel, (fields, ry, rz, tiles, nt, slots)),
        out_shape=[rows_of(count)] * 2,
        in_specs=[smem] * 3 + [vmem] * 14,
        out_specs=[vmem, vmem],
        scratch_shapes=[block_of(fields * w * (ext + 2) * store) for w in (tiles, tiles, 2, 2)]
        + [pltpu.VMEM((2, 2, tiles, 2 * ry // 8, 8, LANES), jnp.float32)]
        + [block_of(fields * 2 * tiles * 2 * ry)] * 2,
        compiler_params=pltpu.CompilerParams(vmem_limit_bytes=32 << 20),
        name="steps",
    )(
        turbine_x, turbine_y, yaw_index, own, got_near, got_far, out_own, out_got, in_own, in_near, in_far,
        *fringes,
    )
    back = lax.ppermute(send, "span", across)

    def place(other, block, *earlier):
        return pl.pallas_call(
            functools.partial(place_kernel, dims, other),
            out_shape=rows_of(slots * count),
            in_specs=[vmem] + [hbm] * len(earlier),
            out_specs=hbm,
            scratch_shapes=[block_of(count), pltpu.SemaphoreType.DMA((fields,))],
            input_output_aliases={1: 0} if earlier else {},
            compiler_params=pltpu.CompilerParams(vmem_limit_bytes=8 << 20),
            name="place",
        )(block, *earlier)

    return unflat(place(True, back, place(False, mine)), state.shape)


def extended_2(shard, sides, width):
    for axis, dim in sides:
        size, length = (lax.axis_size(axis), shard.shape[dim])
        up = [(i, (i + 1) % size) for i in range(size)]
        down = [(j, i) for i, j in up]
        last = lax.slice_in_dim(shard, length - width, length, axis=dim)
        leading = lax.slice_in_dim(shard, 0, width, axis=dim)
        before = lax.ppermute(last, axis, up)
        after = lax.ppermute(leading, axis, down)
        shard = jnp.concatenate([before, shard, after], axis=dim)
    return shard


def entering(part, axis, combine, identity):
    place = lax.axis_index(axis)
    gathered = jax.tree.map(lambda a: lax.all_gather(a, axis), part)
    state = jax.tree.map(lambda a, e: jnp.zeros_like(a) + jnp.asarray(e, a.dtype), part, identity)

    def one(step, state):
        return combine(
            state, jax.tree.map(lambda a: lax.dynamic_index_in_dim(a, step, 0, False), gathered)
        )

    return lax.fori_loop(0, place, one, state)


def tendency(center, east, west, north, south, upper, lower, weight, cos_yaw, sin_yaw):
    grad_x = (east - west) * 0.5
    grad_y = (north - south) * 0.5
    grad_z = (upper - lower) * 0.5
    laplace = east + west + north + south + upper + lower - 6.0 * center
    vel_u = center[..., 1, :, :, :]
    vel_v = center[..., 2, :, :, :]
    vel_w = center[..., 3, :, :, :]
    dux = grad_x[..., 1, :, :, :]
    dvy = grad_y[..., 2, :, :, :]
    dwz = grad_z[..., 3, :, :, :]
    duy = grad_y[..., 1, :, :, :]
    duz = grad_z[..., 1, :, :, :]
    strain = dux * dux + dvy * dvy + dwz * dwz + duy * duy + duz * duz
    viscous = VISC * jnp.sqrt(1.0 + strain)
    speed = U_MEAN + vel_u
    flow = -(
        jnp.expand_dims(speed, -4) * grad_x
        + jnp.expand_dims(vel_v, -4) * grad_y
        + jnp.expand_dims(vel_w, -4) * grad_z
    )
    flow = flow + jnp.expand_dims(viscous, -4) * laplace
    normal = speed * cos_yaw + vel_v * sin_yaw
    thrust = THRUST * normal * jnp.abs(normal) * weight
    extra = jnp.stack(
        [
            -(dux + dvy + dwz),
            -grad_x[..., 0, :, :, :] - thrust * cos_yaw,
            -grad_y[..., 0, :, :, :] - thrust * sin_yaw,
            -grad_z[..., 0, :, :, :],
        ],
        axis=-4,
    )
    return flow + extra


def extended(fields):
    padded = extended_2(fields, (("span", 2), ("vert", 3)), 1)
    vert_at = lax.axis_index("vert")
    bottom = jnp.where(vert_at == 0, 0.0, padded[:, :, :, :1, :])
    summit = jnp.where(vert_at == lax.axis_size("vert") - 1, 0.0, padded[:, :, :, -1:, :])
    padded = jnp.concatenate([bottom, padded[:, :, :, 1:-1, :], summit], axis=3)
    return padded


def stencil(fields, padded, weight, cos_yaw, sin_yaw):
    east = jnp.roll(fields, -1, axis=4)
    west = jnp.roll(fields, 1, axis=4)
    north = padded[:, :, 2:, 1:-1, :]
    south = padded[:, :, :-2, 1:-1, :]
    upper = padded[:, :, 1:-1, 2:, :]
    lower = padded[:, :, 1:-1, :-2, :]
    return tendency(fields, east, west, north, south, upper, lower, weight, cos_yaw, sin_yaw)


def rate(fields, weight, cos_yaw, sin_yaw):
    return stencil(fields, extended(fields), weight, cos_yaw, sin_yaw)


def make_weight(turbine_x, turbine_y, along_y, along_z, total_y, total_z, active, length):
    along_x = jnp.arange(length, dtype=jnp.int32)
    hit_x = (along_x[None, None, :] == turbine_x[:, :, None]).astype(jnp.float32)
    hit_y = ((along_y[None, None, :] - turbine_y[:, :, None]) % total_y < DISK).astype(jnp.float32)
    plane = jnp.einsum("dky,dkx->dyx", hit_y, hit_x, precision=lax.Precision.HIGHEST)
    lower_half = (along_z < total_z // 2).astype(jnp.float32)
    return plane[:, :, None, :] * lower_half[None, None, :, None] * active[:, None, None, None]


def first_held(earlier, later):
    keep = earlier[1] > 0.0
    return (jnp.where(keep, earlier[0], later[0]), jnp.maximum(earlier[1], later[1]))


def body_general(state, turbine_x, turbine_y, yaw_index):
    slots = state.shape[0]
    rows_y = state.shape[2]
    rows_z = state.shape[3]
    total_y = rows_y * lax.axis_size("span")
    total_z = rows_z * lax.axis_size("vert")
    domain = lax.axis_index("case") * slots + jnp.arange(slots, dtype=jnp.int32)
    active = (domain > 0).astype(jnp.float32)
    along_y = lax.axis_index("span") * rows_y + jnp.arange(rows_y, dtype=jnp.int32)
    along_z = lax.axis_index("vert") * rows_z + jnp.arange(rows_z, dtype=jnp.int32)
    weight = make_weight(turbine_x, turbine_y, along_y, along_z, total_y, total_z, active, state.shape[4])
    angle = (yaw_index.astype(jnp.float32) - 3.5) * YAW_STEP
    cos_yaw = jnp.cos(angle)[:, None, None, None]
    sin_yaw = jnp.sin(angle)[:, None, None, None]
    width = state.shape[4] // 4
    ramp = 0.5 * (1.0 - jnp.cos(jnp.pi * (jnp.arange(width, dtype=jnp.float32) + 1.0) / width))
    case_at = lax.axis_index("case")
    for _ in range(STEPS):
        first = rate(state, weight, cos_yaw, sin_yaw)
        middle = state + TIME_STEP * first
        second = rate(middle, weight, cos_yaw, sin_yaw)
        state = state + 0.5 * TIME_STEP * (first + second)
        front = state[..., :width]
        own_fringe = front[0]
        marker = jnp.ones((), jnp.float32)
        blank = (jnp.zeros_like(own_fringe), jnp.zeros((), jnp.float32))
        passed = entering((own_fringe, marker), "case", first_held, blank)
        source = jnp.where(case_at == 0, own_fringe, passed[0])
        front = front + ramp * (source[None] - front)
        state = jnp.concatenate([front, state[..., width:]], axis=4)
    return state


def body_any(state, turbine_x, turbine_y, yaw_index):
    slots, _, ry, rz, x = state.shape
    fits = lax.axis_size("span") == 2 and slots == 2 and lax.axis_size("vert") % 2 == 0
    fits = fits and ry == 8 and rz % 8 == 0 and x == 4 * LANES
    chosen = body if fits else body_general
    return chosen(state, turbine_x, turbine_y, yaw_index)


def solution(mesh):
    return jax.shard_map(
        body_any,
        mesh=mesh,
        in_specs=(
            P("case", None, "span", "vert", None),
            P("case", None),
            P("case", None),
            P("case"),
        ),
        out_specs=P("case", None, "span", "vert", None),
        check_vma=False,
    )
```

profile of v0, /device:TPU:20, one launch (start us, length us, event | category | flops | bytes accessed | tf_op | source)
XLA Modules:
  0.0 74.7 jit_solution(13510770840448394749)
XLA Ops:
  0.0 1.2 %copy-done = f32[2,4,8,8,512]{4,3,2,1,0:T(8,128)S(1)} copy-done((f32[2,4,8,8,512]{4,3,2,1,0:T(8,128)S(1)}, f32[2,4,8,8,512]{4,3,2,1,0:T(8,128)}, u32[]{:S(2)}) %copy-start) | copy-done | bytes 1048600
  1.2 0.4 away.1
  1.6 0.7 own.1
  2.3 1.3 %collective-permute-start.7 = (f32[288,128]{1,0:T(8,128)S(1)}, f32[288,128]{1,0:T(8,128)S(1)}, u32[]{:S(2)}, u32[]{:S(2)}) collective-permute-start(f32[288,128]{1,0:T(8,128)S(1)} %get-tuple-element.16), channel_id=1, source_target_pairs={{0,16},{1,17},{2,18},{3,19},{4,20},{5,21},{6,22},{7,23}} | collective-permute-start | bytes 442376 | tf_op jit(solution)/shard_map/ppermute | solution.py:358
  3.6 7.1 %collective-permute-done.7 = f32[288,128]{1,0:T(8,128)S(1)} collective-permute-done((f32[288,128]{1,0:T(8,128)S(1)}, f32[288,128]{1,0:T(8,128)S(1)}, u32[]{:S(2)}, u32[]{:S(2)}) %collective-permute-start.7) | collective-permute-done | bytes 147488 | tf_op jit(solution)/shard_map/ppermute | solution.py:358
  10.7 1.3 %collective-permute-start.8 = (f32[288,128]{1,0:T(8,128)S(1)}, f32[288,128]{1,0:T(8,128)S(1)}, u32[]{:S(2)}, u32[]{:S(2)}) collective-permute-start(f32[288,128]{1,0:T(8,128)S(1)} %broadcast_select_fusion), channel_id=1, source_target_pairs={{0,8},{16,24},{1,9},{17,25},{2,10},{18,26},{3,11},{19,27},{4,12},{... | collective-permute-start | bytes 442376 | tf_op jit(solution)/shard_map/ppermute | solution.py:358
  12.0 1.6 %collective-permute-start.1 = (f32[256,128]{1,0:T(8,128)S(1)}, f32[256,128]{1,0:T(8,128)S(1)}, u32[]{:S(2)}, u32[]{:S(2)}) collective-permute-start(f32[256,128]{1,0:T(8,128)S(1)} %get-tuple-element.12.after_ref), channel_id=1, source_target_pairs={{0,4},{4,0},{1,5},{5,1},{2,6},{6,2},{3,7},{7,3},{8,12},{12,8},{9,1... | collective-permute-start | bytes 393224 | tf_op jit(solution)/shard_map/ppermute | solution.py:395
  13.6 0.5 collective-permute-start
  14.1 1.9 %collective-permute-start.2 = (f32[768,128]{1,0:T(8,128)S(1)}, f32[768,128]{1,0:T(8,128)S(1)}, u32[]{:S(2)}, u32[]{:S(2)}) collective-permute-start(f32[768,128]{1,0:T(8,128)S(1)} %get-tuple-element.15), channel_id=1, source_target_pairs={{1,2},{2,1},{5,6},{6,5},{9,10},{10,9},{13,14},{14,13},{17,18},{18,... | collective-permute-start | bytes 1179656 | tf_op jit(solution)/shard_map/ppermute | solution.py:405
  16.2 2.3 %collective-permute-done.1.got_far = f32[256,128]{1,0:T(8,128)S(1)} collective-permute-done((f32[256,128]{1,0:T(8,128)S(1)}, f32[256,128]{1,0:T(8,128)S(1)}, u32[]{:S(2)}, u32[]{:S(2)}) %collective-permute-start.1) | collective-permute-done | bytes 131104 | tf_op jit(solution)/shard_map/ppermute | solution.py:395
  18.5 0.6 collective-permute-start.12
  19.1 5.8 %collective-permute-done.got_near = f32[768,128]{1,0:T(8,128)S(1)} collective-permute-done((f32[768,128]{1,0:T(8,128)S(1)}, f32[768,128]{1,0:T(8,128)S(1)}, u32[]{:S(2)}, u32[]{:S(2)}) %collective-permute-start) | collective-permute-done | bytes 393248 | tf_op jit(solution)/shard_map/ppermute | solution.py:394
  24.9 2.5 %collective-permute-start.3 = (f32[768,128]{1,0:T(8,128)S(1)}, f32[768,128]{1,0:T(8,128)S(1)}, u32[]{:S(2)}, u32[]{:S(2)}) collective-permute-start(f32[768,128]{1,0:T(8,128)S(1)} %collective-permute-done.got_near), channel_id=1, source_target_pairs={{1,2},{2,1},{5,6},{6,5},{9,10},{10,9},{13,14},{14,13},{17,18},{18,... | collective-permute-start | bytes 1179656 | tf_op jit(solution)/shard_map/ppermute | solution.py:409
  27.4 1.6 %collective-permute-start.9 = (f32[288,128]{1,0:T(8,128)S(1)}, f32[288,128]{1,0:T(8,128)S(1)}, u32[]{:S(2)}, u32[]{:S(2)}) collective-permute-start(f32[288,128]{1,0:T(8,128)S(1)} %broadcast_select_fusion.1.p_own), channel_id=1, source_target_pairs={{0,4},{4,0},{1,5},{5,1},{2,6},{6,2},{3,7},{7,3},{8,12},{12,8},{9,1... | collective-permute-start | bytes 442376 | tf_op jit(solution)/shard_map/ppermute | solution.py:408
  29.0 2.7 %collective-permute-start.10 = (f32[288,128]{1,0:T(8,128)S(1)}, f32[288,128]{1,0:T(8,128)S(1)}, u32[]{:S(2)}, u32[]{:S(2)}) collective-permute-start(f32[288,128]{1,0:T(8,128)S(1)} %broadcast_select_fusion.1.p_own), channel_id=1, source_target_pairs={{1,2},{2,1},{5,6},{6,5},{9,10},{10,9},{13,14},{14,13},{17,18},{18,... | collective-permute-start | bytes 442376 | tf_op jit(solution)/shard_map/ppermute | solution.py:415
  31.8 0.9 %collective-permute-done.9.p_got = f32[288,128]{1,0:T(8,128)S(1)} collective-permute-done((f32[288,128]{1,0:T(8,128)S(1)}, f32[288,128]{1,0:T(8,128)S(1)}, u32[]{:S(2)}, u32[]{:S(2)}) %collective-permute-start.9) | collective-permute-done | bytes 147488 | tf_op jit(solution)/shard_map/ppermute | solution.py:408
  32.7 2.9 %collective-permute-done.10.p_out_own = f32[288,128]{1,0:T(8,128)S(1)} collective-permute-done((f32[288,128]{1,0:T(8,128)S(1)}, f32[288,128]{1,0:T(8,128)S(1)}, u32[]{:S(2)}, u32[]{:S(2)}) %collective-permute-start.10) | collective-permute-done | bytes 147488 | tf_op jit(solution)/shard_map/ppermute | solution.py:415
  35.6 2.6 %collective-permute-start.11 = (f32[288,128]{1,0:T(8,128)S(1)}, f32[288,128]{1,0:T(8,128)S(1)}, u32[]{:S(2)}, u32[]{:S(2)}) collective-permute-start(f32[288,128]{1,0:T(8,128)S(1)} %collective-permute-done.9.p_got), channel_id=1, source_target_pairs={{1,2},{2,1},{5,6},{6,5},{9,10},{10,9},{13,14},{14,13},{17,18},{18,... | collective-permute-start | bytes 442376 | tf_op jit(solution)/shard_map/ppermute | solution.py:415
  38.2 3.8 %collective-permute-done.11.p_out_got = f32[288,128]{1,0:T(8,128)S(1)} collective-permute-done((f32[288,128]{1,0:T(8,128)S(1)}, f32[288,128]{1,0:T(8,128)S(1)}, u32[]{:S(2)}, u32[]{:S(2)}) %collective-permute-start.11) | collective-permute-done | bytes 147488 | tf_op jit(solution)/shard_map/ppermute | solution.py:415
  42.1 22.6 %steps.1 = (f32[1024,128]{1,0:T(8,128)S(1)}, f32[1024,128]{1,0:T(8,128)S(1)}) custom-call(s32[2,6]{1,0:T(2,128)S(1)} %copy-done.1, s32[2,6]{1,0:T(2,128)S(1)} %copy-done.2, s32[2]{0:T(128)S(1)} %copy-done.3, f32[1024,128]{1,0:T(8,128)S(1)} %get-tuple-element.13.own, f32[768,128]{1,0:T(8,128)S(1)} %collective-permute-done.got_near, ...), custom_call_target="tpu_custom_call" | custom-call | tf_op jit(solution)/shard_map/steps/pallas_call | solution.py:419
  64.6 1.6 %collective-permute-start.14 = (f32[1024,128]{1,0:T(8,128)S(1)}, f32[1024,128]{1,0:T(8,128)S(1)}, u32[]{:S(2)}, u32[]{:S(2)}) collective-permute-start(f32[1024,128]{1,0:T(8,128)S(1)} %get-tuple-element.17), channel_id=1, source_target_pairs={{0,4},{4,0},{1,5},{5,1},{2,6},{6,2},{3,7},{7,3},{8,12},{12,8},{9,1... | collective-permute-start | bytes 1572872 | tf_op jit(solution)/shard_map/ppermute | solution.py:433
  66.2 0.8 %place.2.refs_1_ = f32[2048,128]{1,0:T(8,128)} custom-call(f32[1024,128]{1,0:T(8,128)S(1)} %get-tuple-element.18.refs_0_), custom_call_target="tpu_custom_call" | custom-call | tf_op jit(solution)/shard_map/place/pallas_call | solution.py:436
  67.0 6.8 %collective-permute-done.14.refs_0_ = f32[1024,128]{1,0:T(8,128)S(1)} collective-permute-done((f32[1024,128]{1,0:T(8,128)S(1)}, f32[1024,128]{1,0:T(8,128)S(1)}, u32[]{:S(2)}, u32[]{:S(2)}) %collective-permute-start.14) | collective-permute-done | bytes 524320 | tf_op jit(solution)/shard_map/ppermute | solution.py:433
  73.9 0.8 %place.3 = f32[2048,128]{1,0:T(8,128)} custom-call(f32[1024,128]{1,0:T(8,128)S(1)} %collective-permute-done.14.refs_0_, f32[2048,128]{1,0:T(8,128)} %place.2.refs_1_), custom_call_target="tpu_custom_call", output_to_operand_aliasing={{}: (1, {})} | custom-call | tf_op jit(solution)/shard_map/place/pallas_call | solution.py:436
  (21 shorter events, 0.2 us)
Async XLA Ops:
  0.0 1.2 %copy-start = (f32[2,4,8,8,512]{4,3,2,1,0:T(8,128)S(1)}, f32[2,4,8,8,512]{4,3,2,1,0:T(8,128)}, u32[]{:S(2)}) copy-start(f32[2,4,8,8,512]{4,3,2,1,0:T(8,128)} %param.4) | copy-start | bytes 3145732
  2.3 8.4 %collective-permute-start.7 = (f32[288,128]{1,0:T(8,128)S(1)}, f32[288,128]{1,0:T(8,128)S(1)}, u32[]{:S(2)}, u32[]{:S(2)}) collective-permute-start(f32[288,128]{1,0:T(8,128)S(1)} %get-tuple-element.16), channel_id=1, source_target_pairs={{0,16},{1,17},{2,18},{3,19},{4,20},{5,21},{6,22},{7,23}} | collective-permute-start | bytes 442376 | tf_op jit(solution)/shard_map/ppermute | solution.py:358
  10.7 7.7 %collective-permute-start.8 = (f32[288,128]{1,0:T(8,128)S(1)}, f32[288,128]{1,0:T(8,128)S(1)}, u32[]{:S(2)}, u32[]{:S(2)}) collective-permute-start(f32[288,128]{1,0:T(8,128)S(1)} %broadcast_select_fusion), channel_id=1, source_target_pairs={{0,8},{16,24},{1,9},{17,25},{2,10},{18,26},{3,11},{19,27},{4,12},{... | collective-permute-start | bytes 442376 | tf_op jit(solution)/shard_map/ppermute | solution.py:358
  12.0 6.4 %collective-permute-start.1 = (f32[256,128]{1,0:T(8,128)S(1)}, f32[256,128]{1,0:T(8,128)S(1)}, u32[]{:S(2)}, u32[]{:S(2)}) collective-permute-start(f32[256,128]{1,0:T(8,128)S(1)} %get-tuple-element.12.after_ref), channel_id=1, source_target_pairs={{0,4},{4,0},{1,5},{5,1},{2,6},{6,2},{3,7},{7,3},{8,12},{12,8},{9,1... | collective-permute-start | bytes 393224 | tf_op jit(solution)/shard_map/ppermute | solution.py:395
  13.6 11.3 %collective-permute-start = (f32[768,128]{1,0:T(8,128)S(1)}, f32[768,128]{1,0:T(8,128)S(1)}, u32[]{:S(2)}, u32[]{:S(2)}) collective-permute-start(f32[768,128]{1,0:T(8,128)S(1)} %get-tuple-element.14), channel_id=1, source_target_pairs={{0,4},{4,0},{1,5},{5,1},{2,6},{6,2},{3,7},{7,3},{8,12},{12,8},{9,1... | collective-permute-start | bytes 1179656 | tf_op jit(solution)/shard_map/ppermute | solution.py:394
  14.1 13.3 %collective-permute-start.2 = (f32[768,128]{1,0:T(8,128)S(1)}, f32[768,128]{1,0:T(8,128)S(1)}, u32[]{:S(2)}, u32[]{:S(2)}) collective-permute-start(f32[768,128]{1,0:T(8,128)S(1)} %get-tuple-element.15), channel_id=1, source_target_pairs={{1,2},{2,1},{5,6},{6,5},{9,10},{10,9},{13,14},{14,13},{17,18},{18,... | collective-permute-start | bytes 1179656 | tf_op jit(solution)/shard_map/ppermute | solution.py:405
  16.0 22.2 %collective-permute-start.4 = (f32[1024,128]{1,0:T(8,128)S(1)}, f32[1024,128]{1,0:T(8,128)S(1)}, u32[]{:S(2)}, u32[]{:S(2)}) collective-permute-start(f32[1024,128]{1,0:T(8,128)S(1)} %get-tuple-element.13.own), channel_id=1, source_target_pairs={{0,1},{1,0},{2,3},{3,2},{4,5},{5,4},{6,7},{7,6},{8,9},{9,8},{10,11... | collective-permute-start | bytes 1572872 | tf_op jit(solution)/shard_map/ppermute | solution.py:406
  16.1 25.9 %copy-start.1 = (s32[2,6]{1,0:T(2,128)S(1)}, s32[2,6]{1,0:T(2,128)}, u32[]{:S(2)}) copy-start(s32[2,6]{1,0:T(2,128)} %xs.1) | copy-start | bytes 148
  16.1 25.9 %copy-start.2 = (s32[2,6]{1,0:T(2,128)S(1)}, s32[2,6]{1,0:T(2,128)}, u32[]{:S(2)}) copy-start(s32[2,6]{1,0:T(2,128)} %ys.1) | copy-start | bytes 148
  16.2 25.9 %copy-start.3 = (s32[2]{0:T(128)S(1)}, s32[2]{0:T(128)}, u32[]{:S(2)}) copy-start(s32[2]{0:T(128)} %yaws.1) | copy-start | bytes 28
  18.5 6.4 %collective-permute-start.6 = (f32[256,128]{1,0:T(8,128)S(1)}, f32[256,128]{1,0:T(8,128)S(1)}, u32[]{:S(2)}, u32[]{:S(2)}) collective-permute-start(f32[256,128]{1,0:T(8,128)S(1)} %collective-permute-done.1.got_far), channel_id=1, source_target_pairs={{0,1},{1,0},{2,3},{3,2},{4,5},{5,4},{6,7},{7,6},{8,9},{9,8},{10,11... | collective-permute-start | bytes 393224 | tf_op jit(solution)/shard_map/ppermute | solution.py:411
  18.5 10.5 %collective-permute-start.12 = (f32[288,128]{1,0:T(8,128)S(1)}, f32[288,128]{1,0:T(8,128)S(1)}, u32[]{:S(2)}, u32[]{:S(2)}) collective-permute-start(f32[288,128]{1,0:T(8,128)S(1)} %broadcast_select_fusion.1.p_own), channel_id=1, source_target_pairs={{0,1},{1,0},{2,3},{3,2},{4,5},{5,4},{6,7},{7,6},{8,9},{9,8},{10,11... | collective-permute-start | bytes 442376 | tf_op jit(solution)/shard_map/ppermute | solution.py:415
  24.9 17.1 %collective-permute-start.5 = (f32[768,128]{1,0:T(8,128)S(1)}, f32[768,128]{1,0:T(8,128)S(1)}, u32[]{:S(2)}, u32[]{:S(2)}) collective-permute-start(f32[768,128]{1,0:T(8,128)S(1)} %collective-permute-done.got_near), channel_id=1, source_target_pairs={{0,1},{1,0},{2,3},{3,2},{4,5},{5,4},{6,7},{7,6},{8,9},{9,8},{10,11... | collective-permute-start | bytes 1179656 | tf_op jit(solution)/shard_map/ppermute | solution.py:410
  24.9 17.1 %collective-permute-start.3 = (f32[768,128]{1,0:T(8,128)S(1)}, f32[768,128]{1,0:T(8,128)S(1)}, u32[]{:S(2)}, u32[]{:S(2)}) collective-permute-start(f32[768,128]{1,0:T(8,128)S(1)} %collective-permute-done.got_near), channel_id=1, source_target_pairs={{1,2},{2,1},{5,6},{6,5},{9,10},{10,9},{13,14},{14,13},{17,18},{18,... | collective-permute-start | bytes 1179656 | tf_op jit(solution)/shard_map/ppermute | solution.py:409
  27.4 5.2 %collective-permute-start.9 = (f32[288,128]{1,0:T(8,128)S(1)}, f32[288,128]{1,0:T(8,128)S(1)}, u32[]{:S(2)}, u32[]{:S(2)}) collective-permute-start(f32[288,128]{1,0:T(8,128)S(1)} %broadcast_select_fusion.1.p_own), channel_id=1, source_target_pairs={{0,4},{4,0},{1,5},{5,1},{2,6},{6,2},{3,7},{7,3},{8,12},{12,8},{9,1... | collective-permute-start | bytes 442376 | tf_op jit(solution)/shard_map/ppermute | solution.py:408
  29.0 6.6 %collective-permute-start.10 = (f32[288,128]{1,0:T(8,128)S(1)}, f32[288,128]{1,0:T(8,128)S(1)}, u32[]{:S(2)}, u32[]{:S(2)}) collective-permute-start(f32[288,128]{1,0:T(8,128)S(1)} %broadcast_select_fusion.1.p_own), channel_id=1, source_target_pairs={{1,2},{2,1},{5,6},{6,5},{9,10},{10,9},{13,14},{14,13},{17,18},{18,... | collective-permute-start | bytes 442376 | tf_op jit(solution)/shard_map/ppermute | solution.py:415
  32.7 5.6 %collective-permute-start.13 = (f32[288,128]{1,0:T(8,128)S(1)}, f32[288,128]{1,0:T(8,128)S(1)}, u32[]{:S(2)}, u32[]{:S(2)}) collective-permute-start(f32[288,128]{1,0:T(8,128)S(1)} %collective-permute-done.9.p_got), channel_id=1, source_target_pairs={{0,1},{1,0},{2,3},{3,2},{4,5},{5,4},{6,7},{7,6},{8,9},{9,8},{10,11... | collective-permute-start | bytes 442376 | tf_op jit(solution)/shard_map/ppermute | solution.py:415
  35.6 6.5 %collective-permute-start.11 = (f32[288,128]{1,0:T(8,128)S(1)}, f32[288,128]{1,0:T(8,128)S(1)}, u32[]{:S(2)}, u32[]{:S(2)}) collective-permute-start(f32[288,128]{1,0:T(8,128)S(1)} %collective-permute-done.9.p_got), channel_id=1, source_target_pairs={{1,2},{2,1},{5,6},{6,5},{9,10},{10,9},{13,14},{14,13},{17,18},{18,... | collective-permute-start | bytes 442376 | tf_op jit(solution)/shard_map/ppermute | solution.py:415
  64.6 9.2 %collective-permute-start.14 = (f32[1024,128]{1,0:T(8,128)S(1)}, f32[1024,128]{1,0:T(8,128)S(1)}, u32[]{:S(2)}, u32[]{:S(2)}) collective-permute-start(f32[1024,128]{1,0:T(8,128)S(1)} %get-tuple-element.17), channel_id=1, source_target_pairs={{0,4},{4,0},{1,5},{5,1},{2,6},{6,2},{3,7},{7,3},{8,12},{12,8},{9,1... | collective-permute-start | bytes 1572872 | tf_op jit(solution)/shard_map/ppermute | solution.py:433
where the time goes:
time: 75 us; the launch traced here: 74.7 us
  waiting for transfers between devices  29.7 us (40%)
  Pallas kernels  25.3 us (34%)
  starting transfers between devices  18.2 us (24%)
  local copies, waits for them, and re-layouts  1.24 us (2%)
    pallas_call x1, Pallas kernels, body(): pl.pallas_call(functools.partial(main_kernel, (fields, ry, rz, tiles, nt,...  22.6 us
    ppermute x2, waiting for transfers between devices, spread(): moved = lax.ppermute(value, axis, pairs)  7.07 us
    ppermute x1, waiting for transfers between devices, body(): back = lax.ppermute(send, 'span', across)  6.84 us
    ppermute x4, waiting for transfers between devices, body(): fringes.append(lax.ppermute(a, 'vert', pairs))  6.72 us
    ppermute x4, starting transfers between devices, body(): fringes.append(lax.ppermute(a, 'vert', pairs))  5.94 us
    ppermute x1, waiting for transfers between devices, body(): got_near = lax.ppermute(away_near, 'span', across)  5.84 us
    ppermute x2, starting transfers between devices, spread(): moved = lax.ppermute(value, axis, pairs)  2.59 us
    ppermute x1, starting transfers between devices, body(): out_got = lax.ppermute(got_near, 'vert', outer)  2.52 us
  transfers between devices with their start and end apart: 15, of which 7 were waited for; matrix products, arithmetic and copies ran while one was open for 0% of the time, Pallas kernels for 1%

commit v1 on v0

--- a/solution.py
+++ b/solution.py
@@ -6,6 +6,7 @@
 from jax.experimental import pallas as pl
 from jax.experimental.pallas import tpu as pltpu
 from jax.sharding import PartitionSpec as P
+
 
 STEPS = 3
 DISK = 8
@@ -36,61 +37,58 @@
     return jnp.swapaxes(a, 1, 2).reshape(shape)
 
 
-def away_kernel(dims, state_ref, near_ref, far_ref, block, sem):
+def away_kernel(dims, state_ref, near_ref, far_ref, fringe_ref, block, sems):
     fields, ry, rz, tiles = dims
-    size = fields * ry * tiles * rz
+    part = ry * tiles * rz
+    step = tiles * rz
     slot = 1 - lax.axis_index("span")
     even = lax.axis_index("vert") % 2 == 0
-    start = pl.multiple_of(slot * size, 8)
-    copy = pltpu.make_async_copy(state_ref.at[pl.ds(start, size)], block, sem)
-    copy.start()
-    copy.wait()
+    copies = []
+    for f in range(fields):
+        for other in range(2):
+            source = (slot * fields + f if other else f) * part
+            rows = state_ref.at[pl.ds(pl.multiple_of(source, 8), part)]
+            copies.append(pltpu.make_async_copy(rows, block.at[f, other], sems.at[f, other]))
+            copies[-1].start()
     near = jnp.where(even, 0, rz - HALO)
     far = jnp.where(even, HALO, 0)
-    for ref, low, count in ((near_ref, near, HALO), (far_ref, far, rz - HALO)):
-        for f in range(fields):
-            for t in range(tiles):
-                for k in range(count):
-                    row = (f * ry * tiles + t) * rz + low + k
-                    value = block[pl.ds(row, ry, stride=tiles * rz), :]
-                    ref[pl.ds(((f * tiles + t) * count + k) * ry, ry), :] = value
-
-
-def own_kernel(dims, state_ref, after_ref, own_ref, near_ref, fringe_ref, block, first, sems):
-    del after_ref
-    fields, ry, rz, tiles = dims
-    size = fields * ry * tiles * rz
-    slot = lax.axis_index("span")
-    even = lax.axis_index("vert") % 2 == 0
-    start = pl.multiple_of(slot * size, 8)
-    copy_first = pltpu.make_async_copy(state_ref.at[pl.ds(0, size)], first, sems.at[0])
-    copy_own = pltpu.make_async_copy(state_ref.at[pl.ds(start, size)], block, sems.at[1])
-    copy_first.start()
-    copy_own.start()
-    copy_first.wait()
     lane = lax.broadcasted_iota(jnp.int32, (ry, LANES), 1)
     for f in range(fields):
+        copies[2 * f].wait()
+        first = block.at[f, 0]
         strip = jnp.zeros((ry, LANES), jnp.float32)
         for z in range(rz):
-            row = f * ry * tiles * rz + z
-            step = tiles * rz
             place = f * (rz + 1) + z
-            fringe_ref[pl.ds(place * ry, ry), :] = first[pl.ds(row, ry, stride=step), :]
-            after = first[pl.ds(row + rz, ry, stride=step), :]
-            before = first[pl.ds(row + (tiles - 1) * rz, ry, stride=step), :]
+            fringe_ref[pl.ds(place * ry, ry), :] = first[pl.ds(z, ry, stride=step), :]
+            after = first[pl.ds(z + rz, ry, stride=step), :]
+            before = first[pl.ds(z + (tiles - 1) * rz, ry, stride=step), :]
             both = jnp.where(lane < LANES // 2, after, before)
             both = pltpu.roll(both, (HALO + STRIP * z) % LANES, 1)
             here = (lane >= STRIP * z) & (lane < STRIP * z + 2 * HALO)
             strip = jnp.where(here, both, strip)
         fringe_ref[pl.ds((f * (rz + 1) + rz) * ry, ry), :] = strip
-    copy_own.wait()
+        copies[2 * f + 1].wait()
+        other = block.at[f, 1]
+        for ref, low, count in ((near_ref, near, HALO), (far_ref, far, rz - HALO)):
+            for t in range(tiles):
+                for k in range(count):
+                    value = other[pl.ds(t * rz + low + k, ry, stride=step), :]
+                    ref[pl.ds(((f * tiles + t) * count + k) * ry, ry), :] = value
+
+
+def own_kernel(dims, state_ref, after_ref, own_ref, near_ref):
+    del after_ref
+    fields, ry, rz, tiles = dims
+    size = fields * ry * tiles * rz
+    start = lax.axis_index("span") * size
+    even = lax.axis_index("vert") % 2 == 0
+    near = jnp.where(even, 0, rz - HALO)
     for f in range(fields):
         for t in range(tiles):
             for z in range(rz):
-                row = (f * ry * tiles + t) * rz + z
-                value = block[pl.ds(row, ry, stride=tiles * rz), :]
+                row = start + (f * ry * tiles + t) * rz + z
+                value = state_ref[pl.ds(row, ry, stride=tiles * rz), :]
                 own_ref[pl.ds(((f * tiles + t) * rz + z) * ry, ry), :] = value
-    near = jnp.where(even, 0, rz - HALO)
     for c in range(fields * tiles):
         for k in range(HALO):
             row = pl.multiple_of((c * rz + near + k) * ry, 8)
@@ -382,23 +380,25 @@
     def block_of(n):
         return pltpu.VMEM((n, LANES), jnp.float32)
 
-    away_near, away_far = pl.pallas_call(
+    away_near, away_far, fringe = pl.pallas_call(
         functools.partial(away_kernel, dims),
-        out_shape=[rows_of(near_count), rows_of(count - near_count)],
-        in_specs=[hbm],
-        out_specs=[vmem, vmem],
-        scratch_shapes=[block_of(count), pltpu.SemaphoreType.DMA],
+        out_shape=[rows_of(near_count), rows_of(count - near_count), rows_of(fringe_count)],
+        in_specs=[pl.BlockSpec(memory_space=pltpu.HBM)],
+        out_specs=[vmem] * 3,
+        scratch_shapes=[
+            pltpu.VMEM((fields, 2, count // fields, LANES), jnp.float32),
+            pltpu.SemaphoreType.DMA((fields, 2)),
+        ],
         compiler_params=pltpu.CompilerParams(vmem_limit_bytes=8 << 20),
         name="away",
     )(whole)
     got_near = lax.ppermute(away_near, "span", across)
     got_far = lax.ppermute(away_far, "span", across)
-    own, near, fringe = pl.pallas_call(
+    own, near = pl.pallas_call(
         functools.partial(own_kernel, dims),
-        out_shape=[rows_of(count), rows_of(near_count), rows_of(fringe_count)],
-        in_specs=[hbm, hbm],
-        out_specs=[vmem, vmem, vmem],
-        scratch_shapes=[block_of(count), block_of(count), pltpu.SemaphoreType.DMA((2,))],
+        out_shape=[rows_of(count), rows_of(near_count)],
+        in_specs=[vmem, hbm],
+        out_specs=[vmem] * 2,
         compiler_params=pltpu.CompilerParams(vmem_limit_bytes=8 << 20),
         name="own",
     )(whole, away_far)

time: 75 us -> 76.1 us (1.015)
  Pallas kernels: 25.3 us -> 26.8 us
    pallas_call x1, Pallas kernels: 0.35 us -> 2.24 us  [body(): pl.pallas_call(functools.partial(away_kernel, dims), out_shape=[rows_of(n...]
  transfers between devices with their start and end apart: 15 -> 15, of which waited for: 7 -> 7; matrix products, arithmetic and copies ran while one was open for 0% -> 0% of each run, Pallas kernels for 1% -> 2%
where the time goes in v1:
time: 76.1 us; the launch traced here: 75.9 us
  waiting for transfers between devices  29.3 us (39%)
  Pallas kernels  26.8 us (35%)
  starting transfers between devices  18.3 us (24%)
  local copies, waits for them, and re-layouts  1.25 us (2%)
    pallas_call x1, Pallas kernels, body(): pl.pallas_call(functools.partial(main_kernel, (fields, ry, rz, tiles, nt,...  22.6 us
    ppermute x2, waiting for transfers between devices, spread(): moved = lax.ppermute(value, axis, pairs)  7.07 us
    ppermute x1, waiting for transfers between devices, body(): back = lax.ppermute(send, 'span', across)  6.84 us
    ppermute x4, waiting for transfers between devices, body(): fringes.append(lax.ppermute(a, 'vert', pairs))  6.72 us
    ppermute x4, starting transfers between devices, body(): fringes.append(lax.ppermute(a, 'vert', pairs))  5.94 us
    ppermute x1, waiting for transfers between devices, body(): got_near = lax.ppermute(away_near, 'span', across)  5.84 us
    ppermute x2, starting transfers between devices, spread(): moved = lax.ppermute(value, axis, pairs)  2.59 us
    ppermute x1, starting transfers between devices, body(): out_got = lax.ppermute(got_near, 'vert', outer)  2.52 us
  transfers between devices with their start and end apart: 15, of which 7 were waited for; matrix products, arithmetic and copies ran while one was open for 0% of the time, Pallas kernels for 2%

profile of v1, /device:TPU:20, one launch (start us, length us, event | category | flops | bytes accessed | tf_op | source)
XLA Modules:
  0.0 75.9 jit_solution(3826853792801962742)
XLA Ops:
  0.0 1.2 %copy-done = f32[2,4,8,8,512]{4,3,2,1,0:T(8,128)S(1)} copy-done((f32[2,4,8,8,512]{4,3,2,1,0:T(8,128)S(1)}, f32[2,4,8,8,512]{4,3,2,1,0:T(8,128)}, u32[]{:S(2)}) %copy-start) | copy-done | bytes 1048600
  1.2 2.2 %away.1 = (f32[768,128]{1,0:T(8,128)S(1)}, f32[256,128]{1,0:T(8,128)S(1)}, f32[288,128]{1,0:T(8,128)S(1)}) custom-call(f32[2048,128]{1,0:T(8,128)S(1)} %bitcast.10), custom_call_target="tpu_custom_call" | custom-call | tf_op jit(solution)/shard_map/away/pallas_call | solution.py:383
  3.5 1.3 %collective-permute-start.7 = (f32[288,128]{1,0:T(8,128)S(1)}, f32[288,128]{1,0:T(8,128)S(1)}, u32[]{:S(2)}, u32[]{:S(2)}) collective-permute-start(f32[288,128]{1,0:T(8,128)S(1)} %get-tuple-element.16), channel_id=1, source_target_pairs={{0,16},{1,17},{2,18},{3,19},{4,20},{5,21},{6,22},{7,23}} | collective-permute-start | bytes 442376 | tf_op jit(solution)/shard_map/ppermute | solution.py:356
  4.8 7.1 %collective-permute-done.7 = f32[288,128]{1,0:T(8,128)S(1)} collective-permute-done((f32[288,128]{1,0:T(8,128)S(1)}, f32[288,128]{1,0:T(8,128)S(1)}, u32[]{:S(2)}, u32[]{:S(2)}) %collective-permute-start.7) | collective-permute-done | bytes 147488 | tf_op jit(solution)/shard_map/ppermute | solution.py:356
  11.9 1.3 %collective-permute-start.8 = (f32[288,128]{1,0:T(8,128)S(1)}, f32[288,128]{1,0:T(8,128)S(1)}, u32[]{:S(2)}, u32[]{:S(2)}) collective-permute-start(f32[288,128]{1,0:T(8,128)S(1)} %broadcast_select_fusion), channel_id=1, source_target_pairs={{0,8},{16,24},{1,9},{17,25},{2,10},{18,26},{3,11},{19,27},{4,12},{... | collective-permute-start | bytes 442376 | tf_op jit(solution)/shard_map/ppermute | solution.py:356
  13.2 1.6 %collective-permute-start.1 = (f32[256,128]{1,0:T(8,128)S(1)}, f32[256,128]{1,0:T(8,128)S(1)}, u32[]{:S(2)}, u32[]{:S(2)}) collective-permute-start(f32[256,128]{1,0:T(8,128)S(1)} %get-tuple-element.12.after_ref), channel_id=1, source_target_pairs={{0,4},{4,0},{1,5},{5,1},{2,6},{6,2},{3,7},{7,3},{8,12},{12,8},{9,1... | collective-permute-start | bytes 393224 | tf_op jit(solution)/shard_map/ppermute | solution.py:396
  14.7 0.5 collective-permute-start
  15.3 0.3 own.1
  15.6 1.9 %collective-permute-start.2 = (f32[768,128]{1,0:T(8,128)S(1)}, f32[768,128]{1,0:T(8,128)S(1)}, u32[]{:S(2)}, u32[]{:S(2)}) collective-permute-start(f32[768,128]{1,0:T(8,128)S(1)} %get-tuple-element.15), channel_id=1, source_target_pairs={{1,2},{2,1},{5,6},{6,5},{9,10},{10,9},{13,14},{14,13},{17,18},{18,... | collective-permute-start | bytes 1179656 | tf_op jit(solution)/shard_map/ppermute | solution.py:405
  17.7 1.9 %collective-permute-done.1.got_far = f32[256,128]{1,0:T(8,128)S(1)} collective-permute-done((f32[256,128]{1,0:T(8,128)S(1)}, f32[256,128]{1,0:T(8,128)S(1)}, u32[]{:S(2)}, u32[]{:S(2)}) %collective-permute-start.1) | collective-permute-done | bytes 131104 | tf_op jit(solution)/shard_map/ppermute | solution.py:396
  19.6 0.6 collective-permute-start.12
  20.2 5.8 %collective-permute-done.got_near = f32[768,128]{1,0:T(8,128)S(1)} collective-permute-done((f32[768,128]{1,0:T(8,128)S(1)}, f32[768,128]{1,0:T(8,128)S(1)}, u32[]{:S(2)}, u32[]{:S(2)}) %collective-permute-start) | collective-permute-done | bytes 393248 | tf_op jit(solution)/shard_map/ppermute | solution.py:395
  26.1 2.5 %collective-permute-start.3 = (f32[768,128]{1,0:T(8,128)S(1)}, f32[768,128]{1,0:T(8,128)S(1)}, u32[]{:S(2)}, u32[]{:S(2)}) collective-permute-start(f32[768,128]{1,0:T(8,128)S(1)} %collective-permute-done.got_near), channel_id=1, source_target_pairs={{1,2},{2,1},{5,6},{6,5},{9,10},{10,9},{13,14},{14,13},{17,18},{18,... | collective-permute-start | bytes 1179656 | tf_op jit(solution)/shard_map/ppermute | solution.py:409
  28.6 1.6 %collective-permute-start.9 = (f32[288,128]{1,0:T(8,128)S(1)}, f32[288,128]{1,0:T(8,128)S(1)}, u32[]{:S(2)}, u32[]{:S(2)}) collective-permute-start(f32[288,128]{1,0:T(8,128)S(1)} %broadcast_select_fusion.1.p_own), channel_id=1, source_target_pairs={{0,4},{4,0},{1,5},{5,1},{2,6},{6,2},{3,7},{7,3},{8,12},{12,8},{9,1... | collective-permute-start | bytes 442376 | tf_op jit(solution)/shard_map/ppermute | solution.py:408
  30.2 2.7 %collective-permute-start.10 = (f32[288,128]{1,0:T(8,128)S(1)}, f32[288,128]{1,0:T(8,128)S(1)}, u32[]{:S(2)}, u32[]{:S(2)}) collective-permute-start(f32[288,128]{1,0:T(8,128)S(1)} %broadcast_select_fusion.1.p_own), channel_id=1, source_target_pairs={{1,2},{2,1},{5,6},{6,5},{9,10},{10,9},{13,14},{14,13},{17,18},{18,... | collective-permute-start | bytes 442376 | tf_op jit(solution)/shard_map/ppermute | solution.py:415
  32.9 0.9 %collective-permute-done.9.p_got = f32[288,128]{1,0:T(8,128)S(1)} collective-permute-done((f32[288,128]{1,0:T(8,128)S(1)}, f32[288,128]{1,0:T(8,128)S(1)}, u32[]{:S(2)}, u32[]{:S(2)}) %collective-permute-start.9) | collective-permute-done | bytes 147488 | tf_op jit(solution)/shard_map/ppermute | solution.py:408
  33.8 2.9 %collective-permute-done.10.p_out_own = f32[288,128]{1,0:T(8,128)S(1)} collective-permute-done((f32[288,128]{1,0:T(8,128)S(1)}, f32[288,128]{1,0:T(8,128)S(1)}, u32[]{:S(2)}, u32[]{:S(2)}) %collective-permute-start.10) | collective-permute-done | bytes 147488 | tf_op jit(solution)/shard_map/ppermute | solution.py:415
  36.7 2.6 %collective-permute-start.11 = (f32[288,128]{1,0:T(8,128)S(1)}, f32[288,128]{1,0:T(8,128)S(1)}, u32[]{:S(2)}, u32[]{:S(2)}) collective-permute-start(f32[288,128]{1,0:T(8,128)S(1)} %collective-permute-done.9.p_got), channel_id=1, source_target_pairs={{1,2},{2,1},{5,6},{6,5},{9,10},{10,9},{13,14},{14,13},{17,18},{18,... | collective-permute-start | bytes 442376 | tf_op jit(solution)/shard_map/ppermute | solution.py:415
  39.4 3.8 %collective-permute-done.11.p_out_got = f32[288,128]{1,0:T(8,128)S(1)} collective-permute-done((f32[288,128]{1,0:T(8,128)S(1)}, f32[288,128]{1,0:T(8,128)S(1)}, u32[]{:S(2)}, u32[]{:S(2)}) %collective-permute-start.11) | collective-permute-done | bytes 147488 | tf_op jit(solution)/shard_map/ppermute | solution.py:415
  43.2 22.6 %steps.1 = (f32[1024,128]{1,0:T(8,128)S(1)}, f32[1024,128]{1,0:T(8,128)S(1)}) custom-call(s32[2,6]{1,0:T(2,128)S(1)} %copy-done.2, s32[2,6]{1,0:T(2,128)S(1)} %copy-done.3, s32[2]{0:T(128)S(1)} %copy-done.4, f32[1024,128]{1,0:T(8,128)S(1)} %get-tuple-element.13.own, f32[768,128]{1,0:T(8,128)S(1)} %collective-permute-done.got_near, ...), custom_call_target="tpu_custom_call" | custom-call | tf_op jit(solution)/shard_map/steps/pallas_call | solution.py:419
  65.8 1.6 %collective-permute-start.14 = (f32[1024,128]{1,0:T(8,128)S(1)}, f32[1024,128]{1,0:T(8,128)S(1)}, u32[]{:S(2)}, u32[]{:S(2)}) collective-permute-start(f32[1024,128]{1,0:T(8,128)S(1)} %get-tuple-element.17), channel_id=1, source_target_pairs={{0,4},{4,0},{1,5},{5,1},{2,6},{6,2},{3,7},{7,3},{8,12},{12,8},{9,1... | collective-permute-start | bytes 1572872 | tf_op jit(solution)/shard_map/ppermute | solution.py:433
  67.3 0.8 %place.2.refs_1_ = f32[2048,128]{1,0:T(8,128)} custom-call(f32[1024,128]{1,0:T(8,128)S(1)} %get-tuple-element.18.refs_0_), custom_call_target="tpu_custom_call" | custom-call | tf_op jit(solution)/shard_map/place/pallas_call | solution.py:436
  68.2 6.8 %collective-permute-done.14.refs_0_ = f32[1024,128]{1,0:T(8,128)S(1)} collective-permute-done((f32[1024,128]{1,0:T(8,128)S(1)}, f32[1024,128]{1,0:T(8,128)S(1)}, u32[]{:S(2)}, u32[]{:S(2)}) %collective-permute-start.14) | collective-permute-done | bytes 524320 | tf_op jit(solution)/shard_map/ppermute | solution.py:433
  75.0 0.8 %place.3 = f32[2048,128]{1,0:T(8,128)} custom-call(f32[1024,128]{1,0:T(8,128)S(1)} %collective-permute-done.14.refs_0_, f32[2048,128]{1,0:T(8,128)} %place.2.refs_1_), custom_call_target="tpu_custom_call", output_to_operand_aliasing={{}: (1, {})} | custom-call | tf_op jit(solution)/shard_map/place/pallas_call | solution.py:436
  (23 shorter events, 0.2 us)
Async XLA Ops:
  0.0 1.2 %copy-start = (f32[2,4,8,8,512]{4,3,2,1,0:T(8,128)S(1)}, f32[2,4,8,8,512]{4,3,2,1,0:T(8,128)}, u32[]{:S(2)}) copy-start(f32[2,4,8,8,512]{4,3,2,1,0:T(8,128)} %param.4) | copy-start | bytes 3145732
  1.2 14.0 %copy-start.1 = (f32[2,4,8,8,512]{4,3,2,1,0:T(8,128)S(1)}, f32[2,4,8,8,512]{4,3,2,1,0:T(8,128)}, u32[]{:S(2)}) copy-start(f32[2,4,8,8,512]{4,3,2,1,0:T(8,128)} %param.4) | copy-start | bytes 3145732
  3.5 8.4 %collective-permute-start.7 = (f32[288,128]{1,0:T(8,128)S(1)}, f32[288,128]{1,0:T(8,128)S(1)}, u32[]{:S(2)}, u32[]{:S(2)}) collective-permute-start(f32[288,128]{1,0:T(8,128)S(1)} %get-tuple-element.16), channel_id=1, source_target_pairs={{0,16},{1,17},{2,18},{3,19},{4,20},{5,21},{6,22},{7,23}} | collective-permute-start | bytes 442376 | tf_op jit(solution)/shard_map/ppermute | solution.py:356
  11.9 7.7 %collective-permute-start.8 = (f32[288,128]{1,0:T(8,128)S(1)}, f32[288,128]{1,0:T(8,128)S(1)}, u32[]{:S(2)}, u32[]{:S(2)}) collective-permute-start(f32[288,128]{1,0:T(8,128)S(1)} %broadcast_select_fusion), channel_id=1, source_target_pairs={{0,8},{16,24},{1,9},{17,25},{2,10},{18,26},{3,11},{19,27},{4,12},{... | collective-permute-start | bytes 442376 | tf_op jit(solution)/shard_map/ppermute | solution.py:356
  13.2 6.4 %collective-permute-start.1 = (f32[256,128]{1,0:T(8,128)S(1)}, f32[256,128]{1,0:T(8,128)S(1)}, u32[]{:S(2)}, u32[]{:S(2)}) collective-permute-start(f32[256,128]{1,0:T(8,128)S(1)} %get-tuple-element.12.after_ref), channel_id=1, source_target_pairs={{0,4},{4,0},{1,5},{5,1},{2,6},{6,2},{3,7},{7,3},{8,12},{12,8},{9,1... | collective-permute-start | bytes 393224 | tf_op jit(solution)/shard_map/ppermute | solution.py:396
  14.7 11.3 %collective-permute-start = (f32[768,128]{1,0:T(8,128)S(1)}, f32[768,128]{1,0:T(8,128)S(1)}, u32[]{:S(2)}, u32[]{:S(2)}) collective-permute-start(f32[768,128]{1,0:T(8,128)S(1)} %get-tuple-element.14), channel_id=1, source_target_pairs={{0,4},{4,0},{1,5},{5,1},{2,6},{6,2},{3,7},{7,3},{8,12},{12,8},{9,1... | collective-permute-start | bytes 1179656 | tf_op jit(solution)/shard_map/ppermute | solution.py:395
  15.6 13.0 %collective-permute-start.2 = (f32[768,128]{1,0:T(8,128)S(1)}, f32[768,128]{1,0:T(8,128)S(1)}, u32[]{:S(2)}, u32[]{:S(2)}) collective-permute-start(f32[768,128]{1,0:T(8,128)S(1)} %get-tuple-element.15), channel_id=1, source_target_pairs={{1,2},{2,1},{5,6},{6,5},{9,10},{10,9},{13,14},{14,13},{17,18},{18,... | collective-permute-start | bytes 1179656 | tf_op jit(solution)/shard_map/ppermute | solution.py:405
  17.5 21.8 %collective-permute-start.4 = (f32[1024,128]{1,0:T(8,128)S(1)}, f32[1024,128]{1,0:T(8,128)S(1)}, u32[]{:S(2)}, u32[]{:S(2)}) collective-permute-start(f32[1024,128]{1,0:T(8,128)S(1)} %get-tuple-element.13.own), channel_id=1, source_target_pairs={{0,1},{1,0},{2,3},{3,2},{4,5},{5,4},{6,7},{7,6},{8,9},{9,8},{10,11... | collective-permute-start | bytes 1572872 | tf_op jit(solution)/shard_map/ppermute | solution.py:406
  17.6 25.6 %copy-start.2 = (s32[2,6]{1,0:T(2,128)S(1)}, s32[2,6]{1,0:T(2,128)}, u32[]{:S(2)}) copy-start(s32[2,6]{1,0:T(2,128)} %xs.1) | copy-start | bytes 148
  17.6 25.5 %copy-start.3 = (s32[2,6]{1,0:T(2,128)S(1)}, s32[2,6]{1,0:T(2,128)}, u32[]{:S(2)}) copy-start(s32[2,6]{1,0:T(2,128)} %ys.1) | copy-start | bytes 148
  17.7 25.5 %copy-start.4 = (s32[2]{0:T(128)S(1)}, s32[2]{0:T(128)}, u32[]{:S(2)}) copy-start(s32[2]{0:T(128)} %yaws.1) | copy-start | bytes 28
  19.6 6.4 %collective-permute-start.6 = (f32[256,128]{1,0:T(8,128)S(1)}, f32[256,128]{1,0:T(8,128)S(1)}, u32[]{:S(2)}, u32[]{:S(2)}) collective-permute-start(f32[256,128]{1,0:T(8,128)S(1)} %collective-permute-done.1.got_far), channel_id=1, source_target_pairs={{0,1},{1,0},{2,3},{3,2},{4,5},{5,4},{6,7},{7,6},{8,9},{9,8},{10,11... | collective-permute-start | bytes 393224 | tf_op jit(solution)/shard_map/ppermute | solution.py:411
  19.6 10.5 %collective-permute-start.12 = (f32[288,128]{1,0:T(8,128)S(1)}, f32[288,128]{1,0:T(8,128)S(1)}, u32[]{:S(2)}, u32[]{:S(2)}) collective-permute-start(f32[288,128]{1,0:T(8,128)S(1)} %broadcast_select_fusion.1.p_own), channel_id=1, source_target_pairs={{0,1},{1,0},{2,3},{3,2},{4,5},{5,4},{6,7},{7,6},{8,9},{9,8},{10,11... | collective-permute-start | bytes 442376 | tf_op jit(solution)/shard_map/ppermute | solution.py:415
  26.1 17.1 %collective-permute-start.5 = (f32[768,128]{1,0:T(8,128)S(1)}, f32[768,128]{1,0:T(8,128)S(1)}, u32[]{:S(2)}, u32[]{:S(2)}) collective-permute-start(f32[768,128]{1,0:T(8,128)S(1)} %collective-permute-done.got_near), channel_id=1, source_target_pairs={{0,1},{1,0},{2,3},{3,2},{4,5},{5,4},{6,7},{7,6},{8,9},{9,8},{10,11... | collective-permute-start | bytes 1179656 | tf_op jit(solution)/shard_map/ppermute | solution.py:410
  26.1 17.1 %collective-permute-start.3 = (f32[768,128]{1,0:T(8,128)S(1)}, f32[768,128]{1,0:T(8,128)S(1)}, u32[]{:S(2)}, u32[]{:S(2)}) collective-permute-start(f32[768,128]{1,0:T(8,128)S(1)} %collective-permute-done.got_near), channel_id=1, source_target_pairs={{1,2},{2,1},{5,6},{6,5},{9,10},{10,9},{13,14},{14,13},{17,18},{18,... | collective-permute-start | bytes 1179656 | tf_op jit(solution)/shard_map/ppermute | solution.py:409
  28.6 5.2 %collective-permute-start.9 = (f32[288,128]{1,0:T(8,128)S(1)}, f32[288,128]{1,0:T(8,128)S(1)}, u32[]{:S(2)}, u32[]{:S(2)}) collective-permute-start(f32[288,128]{1,0:T(8,128)S(1)} %broadcast_select_fusion.1.p_own), channel_id=1, source_target_pairs={{0,4},{4,0},{1,5},{5,1},{2,6},{6,2},{3,7},{7,3},{8,12},{12,8},{9,1... | collective-permute-start | bytes 442376 | tf_op jit(solution)/shard_map/ppermute | solution.py:408
  30.2 6.6 %collective-permute-start.10 = (f32[288,128]{1,0:T(8,128)S(1)}, f32[288,128]{1,0:T(8,128)S(1)}, u32[]{:S(2)}, u32[]{:S(2)}) collective-permute-start(f32[288,128]{1,0:T(8,128)S(1)} %broadcast_select_fusion.1.p_own), channel_id=1, source_target_pairs={{1,2},{2,1},{5,6},{6,5},{9,10},{10,9},{13,14},{14,13},{17,18},{18,... | collective-permute-start | bytes 442376 | tf_op jit(solution)/shard_map/ppermute | solution.py:415
  33.8 5.6 %collective-permute-start.13 = (f32[288,128]{1,0:T(8,128)S(1)}, f32[288,128]{1,0:T(8,128)S(1)}, u32[]{:S(2)}, u32[]{:S(2)}) collective-permute-start(f32[288,128]{1,0:T(8,128)S(1)} %collective-permute-done.9.p_got), channel_id=1, source_target_pairs={{0,1},{1,0},{2,3},{3,2},{4,5},{5,4},{6,7},{7,6},{8,9},{9,8},{10,11... | collective-permute-start | bytes 442376 | tf_op jit(solution)/shard_map/ppermute | solution.py:415
  36.7 6.5 %collective-permute-start.11 = (f32[288,128]{1,0:T(8,128)S(1)}, f32[288,128]{1,0:T(8,128)S(1)}, u32[]{:S(2)}, u32[]{:S(2)}) collective-permute-start(f32[288,128]{1,0:T(8,128)S(1)} %collective-permute-done.9.p_got), channel_id=1, source_target_pairs={{1,2},{2,1},{5,6},{6,5},{9,10},{10,9},{13,14},{14,13},{17,18},{18,... | collective-permute-start | bytes 442376 | tf_op jit(solution)/shard_map/ppermute | solution.py:415
  65.8 9.2 %collective-permute-start.14 = (f32[1024,128]{1,0:T(8,128)S(1)}, f32[1024,128]{1,0:T(8,128)S(1)}, u32[]{:S(2)}, u32[]{:S(2)}) collective-permute-start(f32[1024,128]{1,0:T(8,128)S(1)} %get-tuple-element.17), channel_id=1, source_target_pairs={{0,4},{4,0},{1,5},{5,1},{2,6},{6,2},{3,7},{7,3},{8,12},{12,8},{9,1... | collective-permute-start | bytes 1572872 | tf_op jit(solution)/shard_map/ppermute | solution.py:433
